TPU v7x, 256 devices: a whole 4x4x8 slice. The times are simulated.
256 devices in a mesh: env: 4 (over x_lo, core), tm: 64 (over x_hi, z, y).
Axes of the slice: x: 4 (x_hi: 2, x_lo: 2; x = x_hi * 2 + x_lo), y: 4, z: 8, core: 2. Of those that a mesh axis runs over, the one named last changes fastest.
Arguments:
- hidden: bfloat16 [4, 64, 256, 1024], P('env', 'tm'), may hold values from -6 to 6
- done_step: int32 [4, 64], P('env', 'tm'), may hold values from 0 to 255
- alive: int32 [4, 64, 256], P('env', None, 'tm'), may hold values 0 or 1
- targets: float32 [4, 64, 256], P('env', None, 'tm'), may hold values from -6 to 6
- gain_t: float32 [1024], replicated, may hold values from 0.25 to 1.75
- w_qkv_t: bfloat16 [1024, 3072], replicated, may hold values from -5 to 5
- w_out_t: bfloat16 [1024, 1024], replicated, may hold values from -0.1875 to 0.1875
- gain_a: float32 [1024], replicated, may hold values from 0.25 to 1.75
- w_qkv_a: bfloat16 [1024, 3072], P('tm'), may hold values from -5 to 5
- w_out_a: bfloat16 [1024, 1024], P('tm'), may hold values from -0.1875 to 0.1875
- w_value: float32 [1024], replicated, may hold values from -0.1875 to 0.1875
Outputs:
- values: float32 [4, 64, 256], P('env', None, 'tm')
- input_grad: bfloat16 [4, 64, 256, 1024], P('env', 'tm')
- qkv_grad: float32 [1024, 3072], P('tm')
- out_grad: float32 [1024, 1024], P('tm')
Inputs may be any that keep to these rules, and one draw needn't show every extreme that they name: `done_step`: the last step of an agent's first episode in the window; later steps form a new episode.
All inputs are finite; a program needn't handle non-finite values. No bound on the sum of `alive` on one device may be relied on, other than what follows from the above.
Results may differ from a plain program's by a relative error of at most 0.02.
Values may be sent and summed in bfloat16 or wider, within the bound.
A program may use at most 128 MiB of HBM per device.

v0:
```python
import math
import jax
import jax.numpy as jnp
from jax import lax
from jax.sharding import PartitionSpec as P

HEADS = 8


def norm_scale(rows, gain):
    return rows * lax.rsqrt(jnp.mean(rows * rows, axis=-1, keepdims=True) + 1e-06) * gain


def attend(qkv, allowed, head_count, layout):
    width = qkv.shape[-1] // 3
    size = width // head_count
    shape = qkv.shape[:-1] + (head_count, size)
    queries = qkv[..., :width].reshape(shape).astype(jnp.float32)
    key_rows = qkv[..., width : 2 * width].reshape(shape).astype(jnp.float32)
    value_rows = qkv[..., 2 * width :].reshape(shape).astype(jnp.float32)
    if layout == "temporal":
        score_form = "bqhe,bkhe->bhqk"
        mix_form = "bhqk,bkhe->bqhe"
    else:
        score_form = "qbhe,kbhe->bhqk"
        mix_form = "bhqk,kbhe->qbhe"
    scores = jnp.einsum(score_form, queries, key_rows) / math.sqrt(size)
    scores = jnp.where(allowed[:, None], scores, -1e30)
    row_max = jnp.max(scores, axis=-1, keepdims=True)
    weights = jnp.exp(scores - row_max)
    probs = (weights / jnp.sum(weights, axis=-1, keepdims=True)).astype(jnp.bfloat16)
    mixed = jnp.einsum(mix_form, probs.astype(jnp.float32), value_rows)
    return mixed.reshape(qkv.shape[:-1] + (width,))


def temporal_block(rows, done, gain, w_qkv, w_out, head_count):
    batch, length, width = rows.shape
    rows_f = rows.astype(jnp.float32)
    normed = norm_scale(rows_f, gain).astype(jnp.bfloat16)
    qkv = jnp.dot(normed.reshape(-1, width), w_qkv, preferred_element_type=jnp.float32)
    qkv = qkv.astype(jnp.bfloat16).reshape(batch, length, 3 * width)
    positions = jnp.arange(length, dtype=jnp.int32)
    later = positions[None, :] > done[:, None]
    causal = positions[:, None] >= positions[None, :]
    allowed = causal[None] & (later[:, :, None] == later[:, None, :])
    mixed = attend(qkv, allowed, head_count, "temporal").astype(jnp.bfloat16)
    added = jnp.dot(mixed.reshape(-1, width), w_out, preferred_element_type=jnp.float32)
    return (rows_f + added.reshape(batch, length, width)).astype(jnp.bfloat16)


def left_product(left, right):
    return lax.dot_general(
        left, right, (((0,), (0,)), ((), ())), preferred_element_type=jnp.float32
    )


def agent_step(lifted, alive_rows, target_rows, gain, w_qkv, w_out, w_value, head_count):
    agent_count, step_count, width = lifted.shape
    lifted_f = lifted.astype(jnp.float32)
    normed_f, norm_pull = jax.vjp(lambda rows: norm_scale(rows, gain), lifted_f)
    normed = normed_f.astype(jnp.bfloat16).reshape(-1, width)
    qkv = jnp.dot(normed, w_qkv, preferred_element_type=jnp.float32)
    qkv = qkv.astype(jnp.bfloat16).reshape(agent_count, step_count, 3 * width)
    living = alive_rows.T == 1
    allowed = living[:, None, :] | jnp.eye(agent_count, dtype=bool)[None]
    mixed_f, attend_pull = jax.vjp(lambda block: attend(block, allowed, head_count, "agents"), qkv)
    mixed = mixed_f.astype(jnp.bfloat16).reshape(-1, width)
    added = jnp.dot(mixed, w_out, preferred_element_type=jnp.float32)
    top_rows = lifted_f + added.reshape(agent_count, step_count, width)
    predicted = jnp.sum(top_rows * w_value, axis=-1)
    residual_err = 32.0 * alive_rows.astype(jnp.float32) * (predicted - target_rows)
    grad_top = residual_err[..., None] * w_value
    grad_rows = grad_top.astype(jnp.bfloat16).reshape(-1, width)
    grad_mixed = jnp.dot(grad_rows, w_out.T, preferred_element_type=jnp.float32)
    grad_qkv = attend_pull(grad_mixed.reshape(agent_count, step_count, width))[0]
    grad_qkv = grad_qkv.reshape(-1, 3 * width)
    grad_normed = jnp.dot(grad_qkv, w_qkv.T, preferred_element_type=jnp.float32)
    grad_lifted = grad_top + norm_pull(grad_normed.reshape(agent_count, step_count, width))[0]
    return (predicted, grad_lifted.astype(jnp.bfloat16), normed, grad_qkv, mixed, grad_rows)


def per_device(
    hidden, done_step, alive, targets, gain_t, w_qkv_t, w_out_t, gain_a, w_qkv_a, w_out_a, w_value
):
    width = hidden.shape[-1]
    local_rows = hidden[0]
    done_rows = done_step[0]
    first, pull = jax.vjp(
        lambda rows: temporal_block(rows, done_rows, gain_t, w_qkv_t, w_out_t, HEADS), local_rows
    )
    lifted = lax.all_to_all(first, "tm", split_axis=1, concat_axis=0, tiled=True)
    qkv_full, out_full = (
        lax.all_gather(w_qkv_a, "tm", axis=0, tiled=True),
        lax.all_gather(w_out_a, "tm", axis=0, tiled=True),
    )
    predicted, grad_lifted, normed, grad_qkv, mixed, grad_rows = agent_step(
        lifted, alive[0], targets[0], gain_a, qkv_full, out_full, w_value, HEADS
    )
    terms = jnp.concatenate(
        [left_product(normed, grad_qkv), left_product(mixed, grad_rows)], axis=1
    )
    summed = lax.psum_scatter(terms, "tm", scatter_dimension=0, tiled=True)
    totals = lax.psum(summed.astype(jnp.bfloat16), "env").astype(jnp.float32)
    qkv_grad = totals[:, : 3 * width]
    out_grad = totals[:, 3 * width :]
    returned = lax.all_to_all(grad_lifted, "tm", split_axis=0, concat_axis=1, tiled=True)
    input_grad = pull(returned)[0]
    return (predicted[None], input_grad[None], qkv_grad, out_grad)


def solution(mesh):
    in_specs = (
        P("env", "tm", None, None),
        P("env", "tm"),
        P("env", None, "tm"),
        P("env", None, "tm"),
        P(),
        P(),
        P(),
        P(),
        P("tm", None),
        P("tm", None),
        P(),
    )
    out_specs = (P("env", None, "tm"), P("env", "tm", None, None), P("tm", None), P("tm", None))
    return jax.shard_map(
        per_device, mesh=mesh, in_specs=in_specs, out_specs=out_specs, check_vma=False
    )
```

profile of v0, /device:TPU:1, one launch (start us, length us, event | category | flops | bytes accessed | tf_op | source)
XLA Modules:
  0.0 746.1 jit_solution(15809563214694229206)
XLA Ops:
  9.3 1.2 fusion.59
  10.7 4.9 fusion.2
  15.5 0.9 slice_bitcast_fusion
  16.5 0.9 copy.161
  17.6 1.4 copy.155
  22.5 1.9 copy.206
  24.9 5.6 reduce.17
  30.4 2.2 reshape.471
  32.6 15.4 %all-to-all-start = ((bf16[64,2,2048]{2,1,0:T(2,128)(2,1)}), bf16[64,2,2048]{2,1,0:T(2,128)(2,1)}, u32[]{:S(2)}, u32[]{:S(2)}) async-start(bf16[64,2,2048]{2,1,0:T(2,128)(2,1)} %reshape.471), calls=%async_computation | async-start | bytes 1048576 | tf_op jit(solution)/shard_map/all_to_all | solution.py:91
  48.7 16.4 %all-to-all-done = bf16[64,2,2048]{2,1,0:T(2,128)(2,1)} async-done(((bf16[64,2,2048]{2,1,0:T(2,128)(2,1)}), bf16[64,2,2048]{2,1,0:T(2,128)(2,1)}, u32[]{:S(2)}, u32[]{:S(2)}) %all-to-all-start) | async-done | bytes 524320 | tf_op jit(solution)/shard_map/all_to_all | solution.py:91
  65.0 4.5 reshape.472
  69.5 6.9 multiply_reduce_fusion.1
  76.6 2.6 reshape.459
  79.1 3.3 bitcast_convert_fusion
  82.4 69.5 %all-gather.3.cloned.1.call-done = bf16[1024,3072]{1,0:T(8,128)(2,1)} async-done(((bf16[16,3072]{1,0:T(8,128)(2,1)}), bf16[1024,3072]{1,0:T(8,128)(2,1)}) %all-gather.3.cloned.1.call-update) | async-done | bytes 6291472 | tf_op jit(solution)/shard_map/all_gather | solution.py:93
  151.9 6.2 convolution_convert_fusion
  158.1 4.0 reshape.445
  162.1 2.9 fusion.129
  164.9 2.0 reshape.469
  167.0 2.0 reshape.468
  169.0 2.0 reshape.470
  171.0 1.9 fusion.132
  173.2 0.8 copy-done.3
  174.0 1.3 fusion.50
  175.2 95.3 %all-gather.5.cloned.1.call-done = bf16[1024,1024]{1,0:T(8,128)(2,1)} async-done(((bf16[16,1024]{1,0:T(8,128)(2,1)}), bf16[1024,1024]{1,0:T(8,128)(2,1)}) %all-gather.5.cloned.1.call-update) | async-done | bytes 2097168 | tf_op jit(solution)/shard_map/all_gather | solution.py:94
  270.5 3.3 fusion.44
  280.9 0.9 slice-done.3
  282.0 3.5 multiply_reduce_fusion
  285.5 2.5 convolution_bitcast_fusion
  288.0 6.0 pad_maximum_fusion
  294.1 2.2 fusion.60
  296.3 1.2 copy.124
  297.5 7.9 %all-to-all-start.1 = ((bf16[64,4,1024]{2,1,0:T(4,128)(2,1)}), bf16[64,4,1024]{2,1,0:T(4,128)(2,1)}, u32[]{:S(2)}, u32[]{:S(2)}) async-start(bf16[64,4,1024]{2,1,0:T(4,128)(2,1)} %copy.124), calls=%async_computation.1 | async-start | bytes 1048576 | tf_op jit(solution)/shard_map/all_to_all | solution.py:106
  305.5 19.2 %all-to-all-done.1 = bf16[64,4,1024]{2,1,0:T(4,128)(2,1)} async-done(((bf16[64,4,1024]{2,1,0:T(4,128)(2,1)}), bf16[64,4,1024]{2,1,0:T(4,128)(2,1)}, u32[]{:S(2)}, u32[]{:S(2)}) %all-to-all-start.1) | async-done | bytes 524320 | tf_op jit(solution)/shard_map/all_to_all | solution.py:106
  324.8 2.0 all_to_all.8
  326.7 2.6 convolution_convert_fusion.5
  329.3 2.1 copy.142
  331.4 2.7 fusion.6
  334.1 1.0 convert_reduce_fusion
  335.6 1.2 fusion.33
  336.9 1.2 fusion.32
  339.1 2.9 fusion.58
  341.9 309.4 %reduce-scatter.2.cloned.1.call-done = f32[16,4096]{1,0:T(8,128)} async-done(((f32[1024,4096]{1,0:T(8,128)}), f32[16,4096]{1,0:T(8,128)}) %reduce-scatter.2.cloned.1.call-update) | async-done | bytes 262160 | tf_op jit(solution)/shard_map/reduce_scatter | solution.py:102
  651.4 1.6 convert_element_type.264
  653.0 2.3 fusion.76
  655.4 81.0 %all-reduce.8.cloned.1.call-done = bf16[16,4096]{1,0:T(8,128)(2,1)} async-done(((bf16[16,4096]{1,0:T(8,128)(2,1)}), bf16[16,4096]{1,0:T(8,128)(2,1)}) %all-reduce.8.cloned.1.call-update) | async-done | bytes 131088 | tf_op jit(solution)/shard_map/psum | solution.py:103
  736.4 1.4 slice.39
  737.8 1.6 slice.38
  (106 shorter events, 15.4 us)
Async XLA Ops:
  7.2 14.6 %copy-start = (bf16[1024,1024]{1,0:T(8,128)(2,1)S(1)}, bf16[1024,1024]{1,0:T(8,128)(2,1)}, u32[]{:S(2)}) copy-start(bf16[1024,1024]{1,0:T(8,128)(2,1)} %param.17) | copy-start | bytes 6291460
  7.2 144.7 %all-gather.3.cloned.1.call-start = ((), (), s32[]{:S(2)}) async-start(), calls=%async_computation.3 | async-start | bytes 6389760 | tf_op jit(solution)/shard_map/all_gather | solution.py:93
  7.9 262.6 %all-gather.5.cloned.1.call-start = ((), (), s32[]{:S(2)}) async-start(), calls=%async_computation.4 | async-start | bytes 2129920 | tf_op jit(solution)/shard_map/all_gather | solution.py:94
  17.6 2.0 copy-start.10
  19.0 0.8 copy-start.12
  19.6 1.3 copy-start.1
  20.1 1.2 copy-start.7
  20.1 1.6 copy-start.5
  24.3 24.2 %copy-start.19 = (s32[1,64,4]{1,2,0:T(4,128)S(1)}, s32[1,64,4]{1,2,0:T(4,128)}, u32[]{:S(2)}) copy-start(s32[1,64,4]{1,2,0:T(4,128)} %param.13) | copy-start | bytes 3076
  32.6 32.4 %all-to-all-start = ((bf16[64,2,2048]{2,1,0:T(2,128)(2,1)}), bf16[64,2,2048]{2,1,0:T(2,128)(2,1)}, u32[]{:S(2)}, u32[]{:S(2)}) async-start(bf16[64,2,2048]{2,1,0:T(2,128)(2,1)} %reshape.471), calls=%async_computation | async-start | bytes 1048576 | tf_op jit(solution)/shard_map/all_to_all | solution.py:91
  48.0 603.4 %reduce-scatter.2.cloned.1.call-start = ((), (), s32[]{:S(2)}) async-start(), calls=%async_computation.5 | async-start | bytes 17039360 | tf_op jit(solution)/shard_map/reduce_scatter | solution.py:102
  76.6 75.3 %copy-start.24 = (f32[1024]{0:T(1024)S(1)}, f32[1024]{0:T(1024)}, u32[]{:S(2)}) copy-start(f32[1024]{0:T(1024)} %param.18) | copy-start | bytes 12292
  171.0 2.9 copy-start.15
  172.9 1.1 copy-start.3
  174.0 96.6 %copy-start.20 = (f32[1024]{0:T(1024)S(1)}, f32[1024]{0:T(1024)}, u32[]{:S(2)}) copy-start(f32[1024]{0:T(1024)} %param.21) | copy-start | bytes 12292
  175.2 98.6 %copy-start.21 = (f32[1,64,4]{1,2,0:T(4,128)S(1)}, f32[1,64,4]{1,2,0:T(4,128)}, u32[]{:S(2)}) copy-start(f32[1,64,4]{1,2,0:T(4,128)} %param.14) | copy-start | bytes 3076
  270.5 3.4 copy-start.23
  273.9 1.6 copy-start.22
  273.9 1.2 copy-start.4
  275.1 1.0 copy-start.16
  276.2 1.4 copy-start.18
  277.5 1.0 copy-start.17
  278.6 1.0 copy-start.26
  278.6 2.4 slice-start.2
  279.6 2.2 slice-start.3
  280.4 1.6 copy-start.9
  297.5 27.2 %all-to-all-start.1 = ((bf16[64,4,1024]{2,1,0:T(4,128)(2,1)}), bf16[64,4,1024]{2,1,0:T(4,128)(2,1)}, u32[]{:S(2)}, u32[]{:S(2)}) async-start(bf16[64,4,1024]{2,1,0:T(4,128)(2,1)} %copy.124), calls=%async_computation.1 | async-start | bytes 1048576 | tf_op jit(solution)/shard_map/all_to_all | solution.py:106
  305.4 430.9 %all-reduce.8.cloned.1.call-start = ((), (), s32[]{:S(2)}) async-start(), calls=%async_computation.6 | async-start | bytes 262144 | tf_op jit(solution)/shard_map/psum | solution.py:103
  331.4 2.7 copy-start.2
  334.1 1.0 copy-start.8
  334.1 1.5 copy-start.11
  335.6 1.2 copy-start.13
  335.6 2.4 slice-start
  336.9 1.5 copy-start.6
  336.9 2.2 slice-start.1
  336.9 2.2 copy-start.25
  339.1 313.9 %copy-start.14 = (bf16[256,1024]{1,0:T(8,128)(2,1)S(1)}, bf16[256,1024]{1,0:T(8,128)(2,1)}, u32[]{:S(2)}) copy-start(bf16[256,1024]{1,0:T(8,128)(2,1)} %all_to_all.8) | copy-start | bytes 1572868
Sparse Core Ops, SparseCore 0:
  11.7 140.1 all-gather.2
  155.5 114.9 all-gather.4
  294.2 357.0 reduce-scatter.1
  654.4 81.9 all-reduce.7
where the time goes:
time: 755 us; the launch traced here: 746 us
  waiting for transfers between devices  592 us (78%)
  local copies, waits for them, and re-layouts  42.7 us (6%)
  matrix products  40 us (5%)
  other arithmetic  32.1 us (4%)
  starting transfers between devices  23.9 us (3%)
  between operations  15.2 us (2%)
    reduce_scatter x1, waiting for transfers between devices, per_device(): summed = lax.psum_scatter(terms, 'tm', scatter_dimension=0, tiled=True)  309 us
    all_gather x1, waiting for transfers between devices, per_device(): lax.all_gather(w_out_a, 'tm', axis=0, tiled=True)  95.3 us
    psum x1, waiting for transfers between devices, per_device(): totals = lax.psum(summed.astype(jnp.bfloat16), 'env').astype(jnp.float32)  81 us
    all_gather x1, waiting for transfers between devices, per_device(): lax.all_gather(w_qkv_a, 'tm', axis=0, tiled=True)  69.5 us
    all_to_all x1, waiting for transfers between devices, per_device(): lax.all_to_all(grad_lifted, 'tm', split_axis=0, concat_axis=1, tiled=True)  19.2 us
    all_to_all x1, waiting for transfers between devices, per_device(): lax.all_to_all(first, 'tm', split_axis=1, concat_axis=0, tiled=True)  16.4 us
    all_to_all x1, starting transfers between devices, per_device(): lax.all_to_all(first, 'tm', split_axis=1, concat_axis=0, tiled=True)  15.4 us
  transfers between devices with their start and end apart: 6, of which 6 were waited for; matrix products, arithmetic and copies ran while one was open for 11% of the time, Pallas kernels for 0%

commit v1 on v0

--- a/solution.py
+++ b/solution.py
@@ -91,7 +91,9 @@
     lifted = lax.all_to_all(first, "tm", split_axis=1, concat_axis=0, tiled=True)
     qkv_full, out_full = (
         lax.all_gather(w_qkv_a, "tm", axis=0, tiled=True),
-        lax.all_gather(w_out_a, "tm", axis=0, tiled=True),
+        jnp.concatenate(
+            lax.all_to_all(jnp.stack([w_out_a] * lax.axis_size("tm")), "tm", 0, 0), axis=0
+        ),
     )
     predicted, grad_lifted, normed, grad_qkv, mixed, grad_rows = agent_step(
         lifted, alive[0], targets[0], gain_a, qkv_full, out_full, w_value, HEADS

time: 755 us -> 679 us (0.90)
  waiting for transfers between devices: 592 us -> 488 us
  blocking collectives: 0 us -> 33.3 us
  starting transfers between devices: 23.9 us -> 15.3 us
    all_gather x1 -> x0, waiting for transfers between devices: 95.3 us -> none  [per_device(): lax.all_gather(w_out_a, 'tm', axis=0, tiled=True)]
    all_to_all x0 -> x1, blocking collectives: none -> 33.3 us  [per_device(): lax.all_to_all(first, 'tm', split_axis=1, concat_axis=0, tiled=True)]
    all_to_all x1, waiting for transfers between devices: 16.4 us -> 0.01 us  [per_device(): lax.all_to_all(jnp.stack([w_out_a] * lax.axis_size('tm')), 'tm', 0, 0)]
    all_to_all x1, starting transfers between devices: 15.4 us -> 7.24 us  [per_device(): lax.all_to_all(jnp.stack([w_out_a] * lax.axis_size('tm')), 'tm', 0, 0)]
  transfers between devices with their start and end apart: 6 -> 5, of which waited for: 6 -> 4; matrix products, arithmetic and copies ran while one was open for 11% -> 12% of each run, Pallas kernels for 0% -> 0%
where the time goes in v1:
time: 679 us; the launch traced here: 669 us
  waiting for transfers between devices  488 us (72%)
  local copies, waits for them, and re-layouts  43.6 us (6%)
  matrix products  41.6 us (6%)
  blocking collectives  33.3 us (5%)
  other arithmetic  32.1 us (5%)
  starting transfers between devices  15.3 us (2%)
  between operations  15.2 us (2%)
    reduce_scatter x1, waiting for transfers between devices, per_device(): summed = lax.psum_scatter(terms, 'tm', scatter_dimension=0, tiled=True)  310 us
    psum x1, waiting for transfers between devices, per_device(): totals = lax.psum(summed.astype(jnp.bfloat16), 'env').astype(jnp.float32)  80.4 us
    all_gather x1, waiting for transfers between devices, per_device(): lax.all_gather(w_qkv_a, 'tm', axis=0, tiled=True)  76.7 us
    all_to_all x1, blocking collectives, per_device(): lax.all_to_all(first, 'tm', split_axis=1, concat_axis=0, tiled=True)  33.3 us
    all_to_all x1, waiting for transfers between devices, per_device(): lax.all_to_all(grad_lifted, 'tm', split_axis=0, concat_axis=1, tiled=True)  20.7 us
    unnamed x67, local copies, waits for them, and re-layouts  14.4 us
  transfers between devices with their start and end apart: 5, of which 4 were waited for; matrix products, arithmetic and copies ran while one was open for 12% of the time, Pallas kernels for 0%

profile of v1, /device:TPU:1, one launch (start us, length us, event | category | flops | bytes accessed | tf_op | source)
XLA Modules:
  0.0 669.4 jit_solution(3363246298419904241)
XLA Ops:
  8.6 1.2 fusion.50
  9.8 4.9 fusion.2
  14.7 0.9 slice_bitcast_fusion
  15.6 0.9 copy.161
  16.7 1.4 copy.155
  21.7 1.8 copy.206
  24.0 5.6 reduce.17
  29.6 2.2 reshape.479
  31.8 33.3 %all_to_all.26 = bf16[64,2,2048]{2,1,0:T(2,128)(2,1)} all-to-all(bf16[64,2,2048]{2,1,0:T(2,128)(2,1)} %reshape.479), channel_id=1, replica_groups=mesh['env'=4,'tm'=64] {'tm'}, dimensions={0} | all-to-all | bytes 1048576 | tf_op jit(solution)/shard_map/all_to_all | solution.py:91
  65.1 1.6 stack.2
  66.7 7.2 %all-to-all-start.1 = ((bf16[64,16,1024]{2,1,0:T(8,128)(2,1)}), bf16[64,16,1024]{2,1,0:T(8,128)(2,1)}, u32[]{:S(2)}, u32[]{:S(2)}) async-start(bf16[64,16,1024]{2,1,0:T(8,128)(2,1)} %stack.2), calls=%async_computation.1 | async-start | bytes 4194304 | tf_op jit(solution)/shard_map/all_to_all | solution.py:95
  74.6 4.4 reshape.480
  79.1 6.9 %multiply_reduce_fusion.1 = (f32[256]{0:T(256)S(1)}, f32[256,1024]{1,0:T(8,128)}) fusion(bf16[256,1,1024]{2,1,0:T(2,128)(2,1)} %reshape.480), kind=kLoop, calls=%fused_computation.92 | loop fusion | flops 786176 | bytes 1573888 | tf_op jit(solution)/shard_map/jvp()/reduce_sum | solution.py:11
  86.2 2.5 reshape.467
  88.8 3.3 bitcast_convert_fusion
  92.0 76.7 %all-gather.2.cloned.1.call-done = bf16[1024,3072]{1,0:T(8,128)(2,1)} async-done(((bf16[16,3072]{1,0:T(8,128)(2,1)}), bf16[1024,3072]{1,0:T(8,128)(2,1)}) %all-gather.2.cloned.1.call-update) | async-done | bytes 6291472 | tf_op jit(solution)/shard_map/all_gather | solution.py:93
  168.8 6.2 convolution_convert_fusion
  175.0 4.0 reshape.452
  179.0 2.9 fusion.120
  181.9 2.0 reshape.477
  183.9 2.0 reshape.476
  185.9 2.0 reshape.478
  188.0 1.9 fusion.123
  190.8 1.2 fusion.41
  192.1 3.2 fusion.37
  195.3 2.4 convolution_bitcast_fusion.2
  203.5 0.9 slice-done.3
  204.6 3.5 multiply_reduce_fusion
  208.1 2.5 convolution_bitcast_fusion
  210.7 6.0 pad_maximum_fusion
  216.7 2.2 fusion.51
  218.9 1.2 copy.124
  220.1 7.5 %all-to-all-start.2 = ((bf16[64,4,1024]{2,1,0:T(4,128)(2,1)}), bf16[64,4,1024]{2,1,0:T(4,128)(2,1)}, u32[]{:S(2)}, u32[]{:S(2)}) async-start(bf16[64,4,1024]{2,1,0:T(4,128)(2,1)} %copy.124), calls=%async_computation.2 | async-start | bytes 1048576 | tf_op jit(solution)/shard_map/all_to_all | solution.py:108
  227.7 20.7 %all-to-all-done.2 = bf16[64,4,1024]{2,1,0:T(4,128)(2,1)} async-done(((bf16[64,4,1024]{2,1,0:T(4,128)(2,1)}), bf16[64,4,1024]{2,1,0:T(4,128)(2,1)}, u32[]{:S(2)}, u32[]{:S(2)}) %all-to-all-start.2) | async-done | bytes 524320 | tf_op jit(solution)/shard_map/all_to_all | solution.py:108
  248.4 2.0 all_to_all.22
  250.4 2.6 convolution_convert_fusion.5
  253.0 2.0 copy.142
  255.0 2.7 fusion.6
  257.7 1.0 convert_reduce_fusion
  259.3 1.2 fusion.26
  260.5 1.2 fusion.25
  262.7 2.9 fusion.49
  265.6 309.6 %reduce-scatter.2.cloned.1.call-done = f32[16,4096]{1,0:T(8,128)} async-done(((f32[1024,4096]{1,0:T(8,128)}), f32[16,4096]{1,0:T(8,128)}) %reduce-scatter.2.cloned.1.call-update) | async-done | bytes 262160 | tf_op jit(solution)/shard_map/reduce_scatter | solution.py:104
  575.2 1.6 convert_element_type.266
  576.8 2.3 fusion.67
  579.2 80.4 %all-reduce.8.cloned.1.call-done = bf16[16,4096]{1,0:T(8,128)(2,1)} async-done(((bf16[16,4096]{1,0:T(8,128)(2,1)}), bf16[16,4096]{1,0:T(8,128)(2,1)}) %all-reduce.8.cloned.1.call-update) | async-done | bytes 131088 | tf_op jit(solution)/shard_map/psum | solution.py:105
  659.6 1.4 slice.39
  661.0 1.6 slice.38
  (105 shorter events, 14.2 us)
Async XLA Ops:
  7.2 13.8 %copy-start = (bf16[1024,1024]{1,0:T(8,128)(2,1)S(1)}, bf16[1024,1024]{1,0:T(8,128)(2,1)}, u32[]{:S(2)}) copy-start(bf16[1024,1024]{1,0:T(8,128)(2,1)} %param.17) | copy-start | bytes 6291460
  7.2 161.6 %all-gather.2.cloned.1.call-start = ((), (), s32[]{:S(2)}) async-start(), calls=%async_computation.4 | async-start | bytes 6389760 | tf_op jit(solution)/shard_map/all_gather | solution.py:93
  16.7 2.1 copy-start.10
  18.1 0.8 copy-start.12
  18.8 1.3 copy-start.1
  19.3 1.4 copy-start.7
  19.3 1.7 copy-start.5
  23.5 41.6 %copy-start.19 = (bf16[16,1024]{1,0:T(8,128)(2,1)S(1)}, bf16[16,1024]{1,0:T(8,128)(2,1)}, u32[]{:S(2)}) copy-start(bf16[16,1024]{1,0:T(8,128)(2,1)} %param.20) | copy-start | bytes 98308
  66.7 7.8 %copy-start.20 = (s32[1,64,4]{1,2,0:T(4,128)S(1)}, s32[1,64,4]{1,2,0:T(4,128)}, u32[]{:S(2)}) copy-start(s32[1,64,4]{1,2,0:T(4,128)} %param.13) | copy-start | bytes 3076
  66.7 125.3 %all-to-all-start.1 = ((bf16[64,16,1024]{2,1,0:T(8,128)(2,1)}), bf16[64,16,1024]{2,1,0:T(8,128)(2,1)}, u32[]{:S(2)}, u32[]{:S(2)}) async-start(bf16[64,16,1024]{2,1,0:T(8,128)(2,1)} %stack.2), calls=%async_computation.1 | async-start | bytes 4194304 | tf_op jit(solution)/shard_map/all_to_all | solution.py:95
  74.0 501.2 %reduce-scatter.2.cloned.1.call-start = ((), (), s32[]{:S(2)}) async-start(), calls=%async_computation.5 | async-start | bytes 17039360 | tf_op jit(solution)/shard_map/reduce_scatter | solution.py:104
  86.2 82.5 %copy-start.24 = (f32[1024]{0:T(1024)S(1)}, f32[1024]{0:T(1024)}, u32[]{:S(2)}) copy-start(f32[1024]{0:T(1024)} %param.18) | copy-start | bytes 12292
  188.0 2.8 copy-start.15
  189.8 1.0 copy-start.3
  190.8 1.3 copy-start.21
  192.1 3.2 copy-start.22
  195.3 2.8 copy-start.23
  195.3 2.5 copy-start.4
  197.7 1.0 copy-start.16
  198.8 1.4 copy-start.18
  200.1 1.0 copy-start.17
  201.2 1.0 copy-start.26
  201.2 2.4 slice-start.2
  202.2 2.2 slice-start.3
  203.0 1.6 copy-start.9
  220.1 28.3 %all-to-all-start.2 = ((bf16[64,4,1024]{2,1,0:T(4,128)(2,1)}), bf16[64,4,1024]{2,1,0:T(4,128)(2,1)}, u32[]{:S(2)}, u32[]{:S(2)}) async-start(bf16[64,4,1024]{2,1,0:T(4,128)(2,1)} %copy.124), calls=%async_computation.2 | async-start | bytes 1048576 | tf_op jit(solution)/shard_map/all_to_all | solution.py:108
  227.6 432.0 %all-reduce.8.cloned.1.call-start = ((), (), s32[]{:S(2)}) async-start(), calls=%async_computation.6 | async-start | bytes 262144 | tf_op jit(solution)/shard_map/psum | solution.py:105
  255.0 2.7 copy-start.2
  257.7 1.0 copy-start.8
  257.7 1.5 copy-start.11
  259.3 1.2 copy-start.13
  259.3 2.4 slice-start
  260.5 1.5 copy-start.6
  260.5 2.2 slice-start.1
  260.5 2.2 copy-start.25
  262.7 314.1 %copy-start.14 = (bf16[256,1024]{1,0:T(8,128)(2,1)S(1)}, bf16[256,1024]{1,0:T(8,128)(2,1)}, u32[]{:S(2)}) copy-start(bf16[256,1024]{1,0:T(8,128)(2,1)} %all_to_all.22) | copy-start | bytes 1572868
Sparse Core Ops, SparseCore 0:
  11.7 156.9 all-gather.1
  216.8 358.2 reduce-scatter.1
  578.4 81.1 all-reduce.7
